TPU v7x, 32 devices: a whole 2x2x4 slice. The times are simulated.
32 devices in a mesh: axial: 16 (over z, y, core), trans: 2 (over x).
Axes of the slice: x: 2, y: 2, z: 4, core: 2. Of those that a mesh axis runs over, the one named last changes fastest.
Arguments:
- source: float32 [128, 512, 512], P('axial', 'trans'), may hold values from -6 to 6
- labels: int32 [128, 512, 512], P('axial', 'trans'), may hold values from 0 to 3
- voltages: float32 [4], replicated, may hold values from -2 to 2
- relax: float32 [2, 512], replicated, may hold values from 0.3 to 1
Outputs:
- potential: float32 [128, 512, 512], P('axial', 'trans')
All inputs are finite; a program needn't handle non-finite values.
Results may differ from a plain program's by a relative error of at most 0.00008.
Values sent between devices are 32-bit elements; how exact they have to be, the bound alone decides.
No kernel may reach another device: no remote copies, remote signals or barrier semaphores. Data moves between devices by JAX's collectives and lax.ppermute only.
A program may use at most 128 MiB of HBM per device.

v0:
```python
import jax
import jax.numpy as jnp
from jax import lax
from jax.sharding import PartitionSpec as P

NX = 512
NY = 512


def from_partner(block, axis, bit):
    count = lax.axis_size(axis)
    route = []
    for low in range(count):
        high = low | 1 << bit
        if high != low and high < count:
            route += [(low, high), (high, low)]
    return lax.ppermute(block, axis, route)


def padded_2(shard, sides, width):
    for axis, dim in sides:
        count, length = (lax.axis_size(axis), shard.shape[dim])
        up = [(i, (i + 1) % count) for i in range(count - 1)]
        down = [(j, i) for i, j in up]
        last = lax.slice_in_dim(shard, length - width, length, axis=dim)
        initial = lax.slice_in_dim(shard, 0, width, axis=dim)
        before = lax.ppermute(last, axis, up)
        after = lax.ppermute(initial, axis, down)
        shard = jnp.concatenate([before, shard, after], axis=dim)
    return shard


def sine_table(count):
    index = jnp.arange(count, dtype=jnp.float32)
    scale = jnp.sqrt(2.0 / (count + 1.0))
    basis = scale * jnp.sin(
        jnp.pi * (index[:, None] + 1.0) * (index[None, :] + 1.0) / (count + 1.0)
    )
    eigen = 2.0 - 2.0 * jnp.cos(jnp.pi * (index + 1.0) / (count + 1.0))
    return (basis, eigen)


def mirror_in(slab):
    ax_count = lax.axis_size("axial")
    digits = ax_count.bit_length() - 1
    for bit in range(digits):
        slab = from_partner(slab, "axial", bit)
    return slab


def mirror_out(slab):
    ax_count = lax.axis_size("axial")
    digits = ax_count.bit_length() - 1
    for bit in range(digits):
        slab = from_partner(slab, "axial", bit)
    return slab


def on_device(source, labels, voltages, relax):
    high = lax.Precision.HIGHEST
    rows = source.shape[1]
    ax_count = lax.axis_size("axial")
    position = lax.axis_index("axial")
    lower = position < ax_count // 2
    basis_x, eigen_x = sine_table(NX)
    basis_y, eigen_y = sine_table(NY)
    row_start = lax.axis_index("trans") * rows
    columns = lax.dynamic_slice_in_dim(basis_x, row_start, rows, 1)
    charge = source
    for region in range(voltages.shape[0]):
        charge = charge + jnp.where(labels == region, voltages[region], 0.0)
    mirrored = mirror_in(charge)[::-1]
    folded = jnp.where(lower, 0.5 * (charge + mirrored), 0.5 * (charge - mirrored))
    inner = jnp.einsum("zxy,jy->zxj", folded, basis_y, precision=high)
    modes = lax.psum(jnp.einsum("kx,zxj->kzj", columns, inner, precision=high), "trans")
    weight_even = relax[0]
    weight_odd = relax[1]
    weight = jnp.where(lower, weight_even, weight_odd)[:, None, None]
    diag = eigen_x[:, None, None] + eigen_y[None, None, :] + 2.0
    first = weight * modes / diag
    padded = padded_2(first, (("axial", 1),), 1)
    below = padded[:, :-2]
    above = padded[:, 2:]
    second = first + weight * (modes - diag * first + below + above) / diag
    back = jnp.einsum("kzj,jy->kzy", second, basis_y, precision=high)
    field = jnp.einsum("kx,kzy->zxy", columns, back, precision=high)
    partner = mirror_out(field)[::-1]
    return field + jnp.where(lower, -1.0, 1.0) * partner


def solution(mesh):
    placed = (P("axial", "trans", None), P("axial", "trans", None), P(), P())
    return jax.shard_map(
        on_device, mesh=mesh, in_specs=placed, out_specs=P("axial", "trans", None), check_vma=False
    )
```

profile of v0, /device:TPU:0, one launch (start us, length us, event | category | flops | bytes accessed | tf_op | source)
XLA Modules:
  0.0 1099.4 jit_solution(4861309574738589126)
XLA Ops:
  6.5 1.5 fusion.42
  8.0 6.9 select_add_fusion
  14.9 2.0 copy-done
  17.4 6.8 collective-permute-done
  24.1 2.9 collective-permute-start.1
  27.0 90.9 %collective-permute-done.1 = f32[8,256,512]{2,1,0:T(8,128)S(1)} collective-permute-done((f32[8,256,512]{2,1,0:T(8,128)S(1)}, f32[8,256,512]{2,1,0:T(8,128)S(1)}, u32[]{:S(2)}, u32[]{:S(2)}) %collective-permute-start.1) | collective-permute-done | bytes 4194336 | tf_op jit(solution)/shard_map/ppermute | solution.py:17
  117.9 1.8 collective-permute-start.2
  119.7 90.4 %collective-permute-done.2 = f32[8,256,512]{2,1,0:T(8,128)} collective-permute-done((f32[8,256,512]{2,1,0:T(8,128)S(1)}, f32[8,256,512]{2,1,0:T(8,128)}, u32[]{:S(2)}, u32[]{:S(2)}) %collective-permute-start.2) | collective-permute-done | bytes 4194336 | tf_op jit(solution)/shard_map/ppermute | solution.py:17
  210.1 2.5 collective-permute-start.3
  212.6 3.6 sine_multiply_fusion
  216.2 176.2 %collective-permute-done.3 = f32[8,256,512]{2,1,0:T(8,128)} collective-permute-done((f32[8,256,512]{2,1,0:T(8,128)}, f32[8,256,512]{2,1,0:T(8,128)}, u32[]{:S(2)}, u32[]{:S(2)}) %collective-permute-start.3) | collective-permute-done | bytes 4194336 | tf_op jit(solution)/shard_map/ppermute | solution.py:17
  392.4 4.6 rev.6
  397.0 14.6 %fusion.8 = f32[8,256,512]{2,1,0:T(8,128)S(1)} fusion(f32[8,256,512]{2,1,0:T(8,128)} %copy-done, f32[8,256,512]{2,1,0:T(8,128)} %rev.6, pred[]{:T(512)S(6)} %lt.6, f32[512]{0:T(512)S(1)} %get-tuple-element.11, f32[512]{0:T(512)S(1)} %get-tuple-element.12), kind=kOutput, calls=%fused_computation.11 | convolution fusion | flops 6448480256 | bytes 12587009 | tf_op jit(solution)/shard_map/zxy,jy->zxj/dot_general | solution.py:74
  411.6 9.1 fusion.20
  421.5 198.1 %all-reduce.2.cloned.1.call-done = f32[512,8,512]{2,0,1:T(8,128)} async-done(((f32[512,8,512]{2,0,1:T(8,128)}), f32[512,8,512]{2,0,1:T(8,128)}) %all-reduce.2.cloned.1.call-update) | async-done | bytes 8388624 | tf_op jit(solution)/shard_map/psum | solution.py:75
  619.6 4.9 multiply_divide_fusion
  624.5 3.2 copy-done.2
  627.9 1.8 collective-permute-start.4
  632.0 3.5 collective-permute-done.5
  635.5 40.0 %fusion.5 = f32[512,8,512]{0,2,1:T(8,128)} fusion(f32[512,8,512]{2,0,1:T(8,128)} %copy-done.2, f32[512,1,512]{2,0,1:T(8,128)S(1)} %collective-permute-done.5, f32[512,1,512]{2,0,1:T(8,128)S(1)} %collective-permute-done.4, f32[512,8,512]{2,0,1:T(8,128)} %all-reduce.2.cloned.1.call-done, f32[512,512]{1,0:T(8,128)S(1)} %add_add_fusion, f32[512]{0:T(512)S(1)} %bitcast.20, ...), kind=kOutput, calls=%fused_computation.8 | convolution fusion | flops 12904562688 | bytes 28317696 | tf_op jit(solution)/shard_map/kzj,jy->kzy/dot_general | solution.py:85
  675.5 9.2 convolution_bitcast_fusion
  684.6 2.0 copy-done.1
  686.6 18.9 %collective-permute-start.6 = (f32[8,256,512]{1,2,0:T(8,128)S(1)}, f32[8,256,512]{1,2,0:T(8,128)S(1)}, u32[]{:S(2)}, u32[]{:S(2)}) collective-permute-start(f32[8,256,512]{1,2,0:T(8,128)S(1)} %convolution_bitcast_fusion), channel_id=1, source_target_pairs={{0,2},{2,0},{4,6},{6,4},{8,10},{10,8},{12,14},{14,12},{16,18},{18,... | collective-permute-start | bytes 12582920 | tf_op jit(solution)/shard_map/ppermute | solution.py:17
  705.5 6.8 collective-permute-done.6
  712.3 2.7 collective-permute-start.7
  715.1 90.9 %collective-permute-done.7 = f32[8,256,512]{1,2,0:T(8,128)S(1)} collective-permute-done((f32[8,256,512]{1,2,0:T(8,128)S(1)}, f32[8,256,512]{1,2,0:T(8,128)S(1)}, u32[]{:S(2)}, u32[]{:S(2)}) %collective-permute-start.7) | collective-permute-done | bytes 4194336 | tf_op jit(solution)/shard_map/ppermute | solution.py:17
  805.9 2.3 collective-permute-start.8
  808.3 90.4 %collective-permute-done.8 = f32[8,256,512]{1,2,0:T(8,128)} collective-permute-done((f32[8,256,512]{1,2,0:T(8,128)S(1)}, f32[8,256,512]{1,2,0:T(8,128)}, u32[]{:S(2)}, u32[]{:S(2)}) %collective-permute-start.8) | collective-permute-done | bytes 4194336 | tf_op jit(solution)/shard_map/ppermute | solution.py:17
  898.7 2.7 collective-permute-start.9
  901.3 179.9 %collective-permute-done.9 = f32[8,256,512]{1,2,0:T(8,128)} collective-permute-done((f32[8,256,512]{1,2,0:T(8,128)}, f32[8,256,512]{1,2,0:T(8,128)}, u32[]{:S(2)}, u32[]{:S(2)}) %collective-permute-start.9) | collective-permute-done | bytes 4194336 | tf_op jit(solution)/shard_map/ppermute | solution.py:17
  1081.2 6.0 multiply_add_fusion
  1087.2 5.3 copy.5
  (15 shorter events, 3.7 us)
Async XLA Ops:
  6.5 613.1 %all-reduce.2.cloned.1.call-start = ((), (), s32[]{:S(2)}) async-start(), calls=%async_computation | async-start | bytes 16777216 | tf_op jit(solution)/shard_map/psum | solution.py:75
  14.9 2.0 copy-start
  16.9 7.2 collective-permute-start
  24.1 93.8 %collective-permute-start.1 = (f32[8,256,512]{2,1,0:T(8,128)S(1)}, f32[8,256,512]{2,1,0:T(8,128)S(1)}, u32[]{:S(2)}, u32[]{:S(2)}) collective-permute-start(f32[8,256,512]{2,1,0:T(8,128)S(1)} %collective-permute-done), channel_id=1, source_target_pairs={{0,4},{4,0},{2,6},{6,2},{8,12},{12,8},{10,14},{14,10},{16,20},{20,... | collective-permute-start | bytes 12582920 | tf_op jit(solution)/shard_map/ppermute | solution.py:17
  117.9 92.2 %collective-permute-start.2 = (f32[8,256,512]{2,1,0:T(8,128)S(1)}, f32[8,256,512]{2,1,0:T(8,128)}, u32[]{:S(2)}, u32[]{:S(2)}) collective-permute-start(f32[8,256,512]{2,1,0:T(8,128)S(1)} %collective-permute-done.1), channel_id=1, source_target_pairs={{0,8},{8,0},{2,10},{10,2},{4,12},{12,4},{6,14},{14,6},{16,24},{24,... | collective-permute-start | bytes 12582920 | tf_op jit(solution)/shard_map/ppermute | solution.py:17
  210.1 182.3 %collective-permute-start.3 = (f32[8,256,512]{2,1,0:T(8,128)}, f32[8,256,512]{2,1,0:T(8,128)}, u32[]{:S(2)}, u32[]{:S(2)}) collective-permute-start(f32[8,256,512]{2,1,0:T(8,128)} %collective-permute-done.2), channel_id=1, source_target_pairs={{0,16},{16,0},{2,18},{18,2},{4,20},{20,4},{6,22},{22,6},{8,24},{24... | collective-permute-start | bytes 12582920 | tf_op jit(solution)/shard_map/ppermute | solution.py:17
  420.7 0.7 copy-start.3
  624.5 3.2 copy-start.2
  627.9 4.0 collective-permute-start.4
  629.8 5.7 collective-permute-start.5
  684.6 2.0 copy-start.1
  686.6 25.7 %collective-permute-start.6 = (f32[8,256,512]{1,2,0:T(8,128)S(1)}, f32[8,256,512]{1,2,0:T(8,128)S(1)}, u32[]{:S(2)}, u32[]{:S(2)}) collective-permute-start(f32[8,256,512]{1,2,0:T(8,128)S(1)} %convolution_bitcast_fusion), channel_id=1, source_target_pairs={{0,2},{2,0},{4,6},{6,4},{8,10},{10,8},{12,14},{14,12},{16,18},{18,... | collective-permute-start | bytes 12582920 | tf_op jit(solution)/shard_map/ppermute | solution.py:17
  712.3 93.6 %collective-permute-start.7 = (f32[8,256,512]{1,2,0:T(8,128)S(1)}, f32[8,256,512]{1,2,0:T(8,128)S(1)}, u32[]{:S(2)}, u32[]{:S(2)}) collective-permute-start(f32[8,256,512]{1,2,0:T(8,128)S(1)} %collective-permute-done.6), channel_id=1, source_target_pairs={{0,4},{4,0},{2,6},{6,2},{8,12},{12,8},{10,14},{14,10},{16,20},{20,... | collective-permute-start | bytes 12582920 | tf_op jit(solution)/shard_map/ppermute | solution.py:17
  805.9 92.7 %collective-permute-start.8 = (f32[8,256,512]{1,2,0:T(8,128)S(1)}, f32[8,256,512]{1,2,0:T(8,128)}, u32[]{:S(2)}, u32[]{:S(2)}) collective-permute-start(f32[8,256,512]{1,2,0:T(8,128)S(1)} %collective-permute-done.7), channel_id=1, source_target_pairs={{0,8},{8,0},{2,10},{10,2},{4,12},{12,4},{6,14},{14,6},{16,24},{24,... | collective-permute-start | bytes 12582920 | tf_op jit(solution)/shard_map/ppermute | solution.py:17
  898.7 182.5 %collective-permute-start.9 = (f32[8,256,512]{1,2,0:T(8,128)}, f32[8,256,512]{1,2,0:T(8,128)}, u32[]{:S(2)}, u32[]{:S(2)}) collective-permute-start(f32[8,256,512]{1,2,0:T(8,128)} %collective-permute-done.8), channel_id=1, source_target_pairs={{0,16},{16,0},{2,18},{18,2},{4,20},{20,4},{6,22},{22,6},{8,24},{24... | collective-permute-start | bytes 12582920 | tf_op jit(solution)/shard_map/ppermute | solution.py:17
Sparse Core Ops, SparseCore 0:
  420.8 198.7 all-reduce.1
where the time goes:
time: 1100 us
  waiting for transfers between devices  935 us (85%)
  matrix products  72.8 us (7%)
  starting transfers between devices  37.4 us (3%)
  other arithmetic  21.5 us (2%)
  local copies, waits for them, and re-layouts  19.4 us (2%)
  between operations  13.5 us (1%)
    ppermute x8, waiting for transfers between devices, from_partner(): return lax.ppermute(block, axis, route)  732 us
    psum x1, waiting for transfers between devices, on_device(): lax.psum(jnp.einsum('kx,zxj->kzj', columns, inner, precision=high), 'trans')  198 us
    dot_general x1, matrix products, on_device(): back = jnp.einsum('kzj,jy->kzy', second, basis_y, precision=high)  40 us
    ppermute x8, starting transfers between devices, from_partner(): return lax.ppermute(block, axis, route)  34.3 us
  transfers between devices with their start and end apart: 11, of which 11 were waited for; matrix products, arithmetic and copies ran while one was open for 0% of the time, Pallas kernels for 0%

commit v1 on v0

--- a/solution.py
+++ b/solution.py
@@ -72,7 +72,8 @@
     mirrored = mirror_in(charge)[::-1]
     folded = jnp.where(lower, 0.5 * (charge + mirrored), 0.5 * (charge - mirrored))
     inner = jnp.einsum("zxy,jy->zxj", folded, basis_y, precision=high)
-    modes = lax.psum(jnp.einsum("kx,zxj->kzj", columns, inner, precision=high), "trans")
+    keep_up_the_outputs = lambda message: lax.all_gather(message, "trans").sum(axis=0)
+    modes = keep_up_the_outputs(jnp.einsum("kx,zxj->kzj", columns, inner, precision=high))
     weight_even = relax[0]
     weight_odd = relax[1]
     weight = jnp.where(lower, weight_even, weight_odd)[:, None, None]

time: 1100 us -> 1120 us (1.018)
  other arithmetic: 21.5 us -> 33.6 us
    all_gather x0 -> x1, waiting for transfers between devices: none -> 199 us  [on_device(): lax.all_gather(message, 'trans').sum(axis=0)]
    psum x1 -> x0, waiting for transfers between devices: 198 us -> none  [on_device(): lax.psum(jnp.einsum('kx,zxj->kzj', columns, inner, precision=high), 'trans')]
    reduce_sum x0 -> x1, other arithmetic: none -> 12.1 us  [on_device(): lax.all_gather(message, 'trans').sum(axis=0)]
where the time goes in v1:
time: 1120 us; the launch traced here: 1110 us
  waiting for transfers between devices  936 us (84%)
  matrix products  73.4 us (7%)
  starting transfers between devices  37.4 us (3%)
  other arithmetic  33.6 us (3%)
  local copies, waits for them, and re-layouts  19.4 us (2%)
  between operations  13.7 us (1%)
    ppermute x8, waiting for transfers between devices, from_partner(): return lax.ppermute(block, axis, route)  732 us
    all_gather x1, waiting for transfers between devices, on_device(): lax.all_gather(message, 'trans').sum(axis=0)  199 us
    dot_general x1, matrix products, on_device(): back = jnp.einsum('kzj,jy->kzy', second, basis_y, precision=high)  40 us
    ppermute x8, starting transfers between devices, from_partner(): return lax.ppermute(block, axis, route)  34.3 us
  transfers between devices with their start and end apart: 11, of which 11 were waited for; matrix products, arithmetic and copies ran while one was open for 0% of the time, Pallas kernels for 0%

profile of v1, /device:TPU:0, one launch (start us, length us, event | category | flops | bytes accessed | tf_op | source)
XLA Modules:
  0.0 1113.1 jit_solution(3405950624693349783)
XLA Ops:
  8.0 6.9 select_add_fusion
  14.9 2.0 copy-done
  17.4 6.8 collective-permute-done
  24.1 2.9 collective-permute-start.1
  27.0 90.9 %collective-permute-done.1 = f32[8,256,512]{2,1,0:T(8,128)S(1)} collective-permute-done((f32[8,256,512]{2,1,0:T(8,128)S(1)}, f32[8,256,512]{2,1,0:T(8,128)S(1)}, u32[]{:S(2)}, u32[]{:S(2)}) %collective-permute-start.1) | collective-permute-done | bytes 4194336 | tf_op jit(solution)/shard_map/ppermute | solution.py:17
  117.9 1.8 collective-permute-start.2
  119.7 90.4 %collective-permute-done.2 = f32[8,256,512]{2,1,0:T(8,128)} collective-permute-done((f32[8,256,512]{2,1,0:T(8,128)S(1)}, f32[8,256,512]{2,1,0:T(8,128)}, u32[]{:S(2)}, u32[]{:S(2)}) %collective-permute-start.2) | collective-permute-done | bytes 4194336 | tf_op jit(solution)/shard_map/ppermute | solution.py:17
  210.1 2.5 collective-permute-start.3
  212.6 3.6 sine_multiply_fusion
  216.2 176.2 %collective-permute-done.3 = f32[8,256,512]{2,1,0:T(8,128)} collective-permute-done((f32[8,256,512]{2,1,0:T(8,128)}, f32[8,256,512]{2,1,0:T(8,128)}, u32[]{:S(2)}, u32[]{:S(2)}) %collective-permute-start.3) | collective-permute-done | bytes 4194336 | tf_op jit(solution)/shard_map/ppermute | solution.py:17
  392.4 4.6 rev.6
  397.0 14.8 %fusion.8 = f32[8,256,512]{2,1,0:T(8,128)S(1)} fusion(f32[8,256,512]{2,1,0:T(8,128)} %copy-done, f32[8,256,512]{2,1,0:T(8,128)} %rev.6, pred[]{:T(512)S(6)} %lt.6, f32[512]{0:T(512)S(1)} %get-tuple-element.11, f32[512]{0:T(512)S(1)} %get-tuple-element.12), kind=kOutput, calls=%fused_computation.11 | convolution fusion | flops 6448480256 | bytes 12587009 | tf_op jit(solution)/shard_map/zxy,jy->zxj/dot_general | solution.py:74
  411.9 9.2 fusion.20
  421.9 198.9 %all-gather.3.cloned.1.call-done = f32[1024,8,512]{2,0,1:T(8,128)} async-done(((f32[512,8,512]{2,0,1:T(8,128)}), f32[1024,8,512]{2,0,1:T(8,128)}) %all-gather.3.cloned.1.call-update) | async-done | bytes 16777232 | tf_op jit(solution)/shard_map/all_gather | solution.py:75
  620.8 12.1 %reduce_sum.9 = f32[512,8,512]{2,0,1:T(8,128)} reduce(f32[2,512,8,512]{3,1,0,2:T(8,128)} %bitcast.20, f32[]{:T(128)} %constant.10.clone.1), dimensions={0}, to_apply=%region_0.1 | reduce | flops 2097152 | bytes 25165828 | tf_op jit(solution)/shard_map/reduce_sum | solution.py:75
  632.9 4.9 multiply_divide_fusion
  637.8 3.2 copy-done.2
  641.2 1.8 collective-permute-start.4
  645.2 3.5 collective-permute-done.5
  648.8 40.0 %fusion.5 = f32[512,8,512]{0,2,1:T(8,128)} fusion(f32[512,8,512]{2,0,1:T(8,128)} %copy-done.2, f32[512,1,512]{2,0,1:T(8,128)S(1)} %collective-permute-done.5, f32[512,1,512]{2,0,1:T(8,128)S(1)} %collective-permute-done.4, f32[512,8,512]{2,0,1:T(8,128)} %reduce_sum.9, f32[512,512]{1,0:T(8,128)S(1)} %add_add_fusion, f32[512]{0:T(512)S(1)} %bitcast.22, ...), kind=kOutput, calls=%fused_computation.8 | convolution fusion | flops 12904562688 | bytes 28317696 | tf_op jit(solution)/shard_map/kzj,jy->kzy/dot_general | solution.py:86
  688.7 9.3 convolution_bitcast_fusion
  698.1 2.0 copy-done.1
  700.1 18.9 %collective-permute-start.6 = (f32[8,256,512]{1,2,0:T(8,128)S(1)}, f32[8,256,512]{1,2,0:T(8,128)S(1)}, u32[]{:S(2)}, u32[]{:S(2)}) collective-permute-start(f32[8,256,512]{1,2,0:T(8,128)S(1)} %convolution_bitcast_fusion), channel_id=1, source_target_pairs={{0,2},{2,0},{4,6},{6,4},{8,10},{10,8},{12,14},{14,12},{16,18},{18,... | collective-permute-start | bytes 12582920 | tf_op jit(solution)/shard_map/ppermute | solution.py:17
  719.0 6.8 collective-permute-done.6
  725.8 2.7 collective-permute-start.7
  728.5 90.9 %collective-permute-done.7 = f32[8,256,512]{1,2,0:T(8,128)S(1)} collective-permute-done((f32[8,256,512]{1,2,0:T(8,128)S(1)}, f32[8,256,512]{1,2,0:T(8,128)S(1)}, u32[]{:S(2)}, u32[]{:S(2)}) %collective-permute-start.7) | collective-permute-done | bytes 4194336 | tf_op jit(solution)/shard_map/ppermute | solution.py:17
  819.4 2.3 collective-permute-start.8
  821.7 90.4 %collective-permute-done.8 = f32[8,256,512]{1,2,0:T(8,128)} collective-permute-done((f32[8,256,512]{1,2,0:T(8,128)S(1)}, f32[8,256,512]{1,2,0:T(8,128)}, u32[]{:S(2)}, u32[]{:S(2)}) %collective-permute-start.8) | collective-permute-done | bytes 4194336 | tf_op jit(solution)/shard_map/ppermute | solution.py:17
  912.1 2.7 collective-permute-start.9
  914.8 179.9 %collective-permute-done.9 = f32[8,256,512]{1,2,0:T(8,128)} collective-permute-done((f32[8,256,512]{1,2,0:T(8,128)}, f32[8,256,512]{1,2,0:T(8,128)}, u32[]{:S(2)}, u32[]{:S(2)}) %collective-permute-start.9) | collective-permute-done | bytes 4194336 | tf_op jit(solution)/shard_map/ppermute | solution.py:17
  1094.7 6.0 multiply_add_fusion
  1100.6 5.3 copy.6
  (16 shorter events, 5.1 us)
Async XLA Ops:
  6.5 614.3 %all-gather.3.cloned.1.call-start = ((), (), s32[]{:S(2)}) async-start(), calls=%async_computation | async-start | bytes 25165824 | tf_op jit(solution)/shard_map/all_gather | solution.py:75
  14.9 2.0 copy-start
  16.9 7.2 collective-permute-start
  24.1 93.8 %collective-permute-start.1 = (f32[8,256,512]{2,1,0:T(8,128)S(1)}, f32[8,256,512]{2,1,0:T(8,128)S(1)}, u32[]{:S(2)}, u32[]{:S(2)}) collective-permute-start(f32[8,256,512]{2,1,0:T(8,128)S(1)} %collective-permute-done), channel_id=1, source_target_pairs={{0,4},{4,0},{2,6},{6,2},{8,12},{12,8},{10,14},{14,10},{16,20},{20,... | collective-permute-start | bytes 12582920 | tf_op jit(solution)/shard_map/ppermute | solution.py:17
  117.9 92.2 %collective-permute-start.2 = (f32[8,256,512]{2,1,0:T(8,128)S(1)}, f32[8,256,512]{2,1,0:T(8,128)}, u32[]{:S(2)}, u32[]{:S(2)}) collective-permute-start(f32[8,256,512]{2,1,0:T(8,128)S(1)} %collective-permute-done.1), channel_id=1, source_target_pairs={{0,8},{8,0},{2,10},{10,2},{4,12},{12,4},{6,14},{14,6},{16,24},{24,... | collective-permute-start | bytes 12582920 | tf_op jit(solution)/shard_map/ppermute | solution.py:17
  210.1 182.3 %collective-permute-start.3 = (f32[8,256,512]{2,1,0:T(8,128)}, f32[8,256,512]{2,1,0:T(8,128)}, u32[]{:S(2)}, u32[]{:S(2)}) collective-permute-start(f32[8,256,512]{2,1,0:T(8,128)} %collective-permute-done.2), channel_id=1, source_target_pairs={{0,16},{16,0},{2,18},{18,2},{4,20},{20,4},{6,22},{22,6},{8,24},{24... | collective-permute-start | bytes 12582920 | tf_op jit(solution)/shard_map/ppermute | solution.py:17
  421.1 0.7 copy-start.3
  637.8 3.2 copy-start.2
  641.2 4.0 collective-permute-start.4
  643.0 5.7 collective-permute-start.5
  698.1 2.0 copy-start.1
  700.1 25.7 %collective-permute-start.6 = (f32[8,256,512]{1,2,0:T(8,128)S(1)}, f32[8,256,512]{1,2,0:T(8,128)S(1)}, u32[]{:S(2)}, u32[]{:S(2)}) collective-permute-start(f32[8,256,512]{1,2,0:T(8,128)S(1)} %convolution_bitcast_fusion), channel_id=1, source_target_pairs={{0,2},{2,0},{4,6},{6,4},{8,10},{10,8},{12,14},{14,12},{16,18},{18,... | collective-permute-start | bytes 12582920 | tf_op jit(solution)/shard_map/ppermute | solution.py:17
  725.8 93.6 %collective-permute-start.7 = (f32[8,256,512]{1,2,0:T(8,128)S(1)}, f32[8,256,512]{1,2,0:T(8,128)S(1)}, u32[]{:S(2)}, u32[]{:S(2)}) collective-permute-start(f32[8,256,512]{1,2,0:T(8,128)S(1)} %collective-permute-done.6), channel_id=1, source_target_pairs={{0,4},{4,0},{2,6},{6,2},{8,12},{12,8},{10,14},{14,10},{16,20},{20,... | collective-permute-start | bytes 12582920 | tf_op jit(solution)/shard_map/ppermute | solution.py:17
  819.4 92.7 %collective-permute-start.8 = (f32[8,256,512]{1,2,0:T(8,128)S(1)}, f32[8,256,512]{1,2,0:T(8,128)}, u32[]{:S(2)}, u32[]{:S(2)}) collective-permute-start(f32[8,256,512]{1,2,0:T(8,128)S(1)} %collective-permute-done.7), channel_id=1, source_target_pairs={{0,8},{8,0},{2,10},{10,2},{4,12},{12,4},{6,14},{14,6},{16,24},{24,... | collective-permute-start | bytes 12582920 | tf_op jit(solution)/shard_map/ppermute | solution.py:17
  912.1 182.5 %collective-permute-start.9 = (f32[8,256,512]{1,2,0:T(8,128)}, f32[8,256,512]{1,2,0:T(8,128)}, u32[]{:S(2)}, u32[]{:S(2)}) collective-permute-start(f32[8,256,512]{1,2,0:T(8,128)} %collective-permute-done.8), channel_id=1, source_target_pairs={{0,16},{16,0},{2,18},{18,2},{4,20},{20,4},{6,22},{22,6},{8,24},{24... | collective-permute-start | bytes 12582920 | tf_op jit(solution)/shard_map/ppermute | solution.py:17
Sparse Core Ops, SparseCore 0:
  421.2 199.5 all-gather.2
